TPU v7x, 512 devices: a whole 4x4x16 slice. The times are simulated.
512 devices in a mesh: phi: 64 (over z, y_hi, core), row: 8 (over y_lo, x).
Axes of the slice: x: 4, y: 4 (y_hi: 2, y_lo: 2; y = y_hi * 2 + y_lo), z: 16, core: 2. Of those that a mesh axis runs over, the one named last changes fastest.
Arguments:
- density: float32 [3, 2, 4096, 1024], P(None, None, 'phi', 'row'), may hold values from 0.5 to 2
- phi_speed: float32 [3, 2, 4096, 1024], P(None, None, 'phi', 'row'), may hold values from -0.3 to 0.3
- rad_speed: float32 [3, 2, 4096, 1024], P(None, None, 'phi', 'row'), may hold values from -0.3 to 0.3
- profile: float32 [2], replicated, may hold values from 0.2 to 1
- tiles: float32 [2, 4096, 8, 1024], P(None, 'phi', None, 'row'), may hold values from -3 to 3
- owners: int32 [2, 4096, 1], P(None, 'phi'), may hold values from 0 to 63; in each aligned block of 64 rows (0 to 63, 64 to 127, ..., all dimensions but the last counted through in order) at most 2 rows name the same one
- slots: int32 [2, 4096], P(None, 'phi'), may hold values from 0 to 7
- shifts: int32 [2, 1024], P(None, 'row'), may hold values from 0 to 4095
Outputs:
- advanced: float32 [3, 2, 4096, 1024], P(None, None, 'phi', 'row')
Inputs may be any that keep to these rules, and one draw needn't show every extreme that they name: `owners`: in each step, among the 64 tiles held by one index of phi, at most 2 name the same owner.
All inputs are finite; a program needn't handle non-finite values.
Results may differ from a plain program's by a relative error of at most 0.000086.
Values sent between devices are 32-bit elements; how exact they have to be, the bound alone decides.
A program may use at most 128 MiB of HBM per device.

v0:
```python
import jax
import jax.numpy as jnp
from jax import lax
from jax.experimental import pallas as pl
from jax.experimental.pallas import tpu as pltpu
from jax.sharding import PartitionSpec as P

MESH = pl.DeviceIdType.MESH


def fold(block):
    turned = block.T
    count = turned.shape[0] // 2
    return jnp.concatenate([turned[:count], turned[count:]], axis=1)


def unfold(block):
    half = block.shape[1] // 2
    return jnp.concatenate([block[:, :half], block[:, half:]], axis=0).T


def fused(
    whole_ref,
    profile_ref,
    rest_ref,
    names_ref,
    mass_ref,
    phi_ref,
    rad_ref,
    tiles_ref,
    out_ref,
    edge_out,
    edge_in,
    names_in,
    tile_out,
    tile_in,
    mass_out,
    mass_in,
    twice,
    held_mass,
    lhs,
    rhs,
    deposit,
    edge_send,
    edge_recv,
    all_send,
    all_recv,
):
    planes, cells, width = mass_ref.shape
    steps = tiles_ref.shape[0]
    strip = tiles_ref.shape[2]
    places = cells // strip
    count, row_count = lax.axis_size("phi"), lax.axis_size("row")
    me, row = lax.axis_index("phi"), lax.axis_index("row")
    lanes = 2 * cells
    up, down = lax.rem(me + 1, count), lax.rem(me + count - 1, count)
    outward, inward = lax.rem(row + 1, row_count), lax.rem(row + row_count - 1, row_count)

    barrier = pltpu.get_barrier_semaphore()

    @pl.loop(1, count)
    def _(step):
        pl.semaphore_signal(barrier, inc=1, device_id={"phi": lax.rem(me + step, count)}, device_id_type=MESH)

    pl.semaphore_signal(barrier, inc=1, device_id={"row": outward}, device_id_type=MESH)
    pl.semaphore_signal(barrier, inc=1, device_id={"row": inward}, device_id_type=MESH)

    def put_column(place, field, column):
        rows = [field[f].T[column : column + 1, :] for f in range(planes)]
        edge_out[place, :planes, :cells] = jnp.concatenate(rows, axis=0)

    def put_row(place, field, at):
        edge_out[place, :planes, :width] = field[:, at, :]

    def edge(place, target):
        return pltpu.make_async_remote_copy(
            src_ref=edge_out.at[place],
            dst_ref=edge_in.at[place],
            send_sem=edge_send.at[place],
            recv_sem=edge_recv.at[place],
            device_id=target,
            device_id_type=MESH,
        )

    def mass_edges(base, field):
        put_row(base, field, cells - 1)
        put_row(base + 1, field, 0)
        put_column(base + 2, field, width - 1)
        put_column(base + 3, field, 0)
        return [
            edge(base, {"phi": up}),
            edge(base + 1, {"phi": down}),
            edge(base + 2, {"row": outward}),
            edge(base + 3, {"row": inward}),
        ]

    def send_all(source, target, number):
        @pl.loop(1, count)
        def _(step):
            peer = lax.rem(me + step, count)
            pltpu.make_async_remote_copy(
                src_ref=source.at[peer],
                dst_ref=target.at[me],
                send_sem=all_send.at[number],
                recv_sem=all_recv.at[number],
                device_id={"phi": peer},
                device_id_type=MESH,
            ).start()

        target[pl.ds(me, 1)] = source[pl.ds(me, 1)]

    def all_wait(target, semaphore):
        others = target.at[pl.ds(0, count - 1)]
        pltpu.make_async_copy(others, others, semaphore).wait()

    density = mass_ref[...]
    first_edges = mass_edges(0, density)
    put_row(8, phi_ref, 0)
    put_column(9, rad_ref, 0)
    first_edges += [edge(8, {"phi": down}), edge(9, {"row": inward})]
    names_in[pl.ds(me, 1)] = names_ref[...]

    pl.semaphore_wait(barrier, count + 1)
    for copy in first_edges:
        copy.start()

    @pl.loop(1, count)
    def _(step):
        pltpu.make_async_remote_copy(
            src_ref=names_ref.at[0],
            dst_ref=names_in.at[me],
            send_sem=all_send.at[0],
            recv_sem=all_recv.at[0],
            device_id={"phi": lax.rem(me + step, count)},
            device_id_type=MESH,
        ).start()

    def send_tiles(number):
        for p in range(strip):
            tile_out[number, :, p, :] = fold(tiles_ref[number, :, p, :])
        send_all(tile_out.at[number], tile_in.at[number], 1 + number)

    send_tiles(0)

    lane = lax.broadcasted_iota(jnp.int32, (1, 1, width), 2)
    cell = lax.broadcasted_iota(jnp.int32, (1, cells, 1), 1)

    def rows_of(place):
        return edge_in[place, :planes, :width].reshape(planes, 1, width)

    def columns_of(place, outside):
        turned = edge_in[place].T
        found = jnp.stack([turned[:cells, f : f + 1] for f in range(planes)], axis=0)
        return jnp.where(outside, 0.0, found)

    for copy in first_edges:
        copy.wait()
    speed_phi, speed_rad = phi_ref[...], rad_ref[...]
    speed_next = jnp.where(cell == cells - 1, rows_of(8), pltpu.roll(speed_phi, cells - 1, 1))
    last_row = row == row_count - 1
    radial_next = jnp.where(lane == width - 1, columns_of(9, last_row), pltpu.roll(speed_rad, width - 1, 2))

    def advance(mass, base):
        behind = jnp.where(cell == 0, rows_of(base), pltpu.roll(mass, 1, 1))
        ahead = jnp.where(cell == cells - 1, rows_of(base + 1), pltpu.roll(mass, cells - 1, 1))
        inner = jnp.where(lane == 0, columns_of(base + 2, row == 0), pltpu.roll(mass, 1, 2))
        outer = jnp.where(lane == width - 1, columns_of(base + 3, last_row), pltpu.roll(mass, width - 1, 2))
        flux_in = jnp.maximum(speed_phi, 0.0) * behind + jnp.minimum(speed_phi, 0.0) * mass
        flux_out = jnp.maximum(speed_next, 0.0) * mass + jnp.minimum(speed_next, 0.0) * ahead
        radial_in = jnp.maximum(speed_rad, 0.0) * inner + jnp.minimum(speed_rad, 0.0) * mass
        radial_out = jnp.maximum(radial_next, 0.0) * mass + jnp.minimum(radial_next, 0.0) * outer
        return mass - (flux_out - flux_in) - (radial_out - radial_in)

    def send_mass(mass, turn, number):
        for f in range(planes):
            mass_out[turn, :, f, :] = fold(mass[f])
        send_all(mass_out.at[turn], mass_in.at[turn], number)

    def make_deposit(number):
        line = lax.broadcasted_iota(jnp.int32, (lanes, lanes), 0)
        spot = lax.broadcasted_iota(jnp.int32, (lanes, lanes), 1)
        same = (line >= cells) == (spot >= cells)
        owner_line = lax.rem(line, cells).astype(jnp.float32)

        deposit[...] = jnp.zeros_like(deposit)

        @pl.loop(0, count // 2)
        def _(pair):
            for side in range(2):
                source = 2 * pair + side
                names = names_in[source]
                own, slot = names[2 * number : 2 * number + 1], names[2 * number + 1 : 2 * number + 2]
                block = tile_in[number, source]
                high = block.astype(jnp.bfloat16).astype(jnp.float32)
                left = block - high
                middle = left.astype(jnp.bfloat16).astype(jnp.float32)
                low = left - middle
                span = slice(side * lanes, (side + 1) * lanes)
                for n, part in enumerate((high, middle, low)):
                    spread = [jnp.where(slot == float(q), part, 0.0) for q in range(places)]
                    rhs[n * cells : (n + 1) * cells, span] = jnp.concatenate(spread, axis=0).astype(jnp.bfloat16)
                hit = jnp.where(same & (own == owner_line), 1.0, 0.0)
                lhs[:, span] = hit.astype(jnp.bfloat16)
            deposit[...] += lax.dot_general(
                lhs[...], rhs[...], (((1,), (1,)), ((), ())), preferred_element_type=jnp.float32
            )

        total = deposit[:, :cells] + deposit[:, cells : 2 * cells] + deposit[:, 2 * cells : 3 * cells]
        return jnp.concatenate([total[:count], total[cells : cells + count]], axis=1)

    spot = lax.broadcasted_iota(jnp.int32, (1, 1, lanes), 2)
    inside = lax.rem(spot, cells)

    def turn_back(source, number, added, turn, channel):
        for f in range(planes):
            block = source[:, f, :]
            if f < profile_ref.shape[0]:
                block = block + profile_ref[f] * added
            twice[pl.ds(1, count), f, :] = block
            twice[pl.ds(1 + count, count), f, :] = block
            twice[0, f : f + 1, :] = block[count - 1 :]
        rest = rest_ref[number : number + 1].reshape(1, 1, lanes)
        low, high = whole_ref[number, 0], whole_ref[number, 1]
        here = jnp.where(spot < cells, twice[pl.ds(1 + count - low, count)], twice[pl.ds(1 + count - high, count)])
        prev = jnp.where(spot < cells, twice[pl.ds(count - low, count)], twice[pl.ds(count - high, count)])
        mixed = jnp.where(inside < cells - rest, here, prev)
        moved = inside - rest
        index = (spot - inside) + jnp.where(moved < 0, moved + cells, moved)
        index = jnp.broadcast_to(index, mixed.shape).reshape(count * planes, lanes)
        mass_out[turn] = jnp.take_along_axis(mixed.reshape(count * planes, lanes), index, axis=1).reshape(mixed.shape)
        send_all(mass_out.at[turn], mass_in.at[turn], channel)

    send_mass(advance(density, 0), 0, 3)
    send_tiles(1)
    all_wait(names_in, all_recv.at[0])
    all_wait(tile_in.at[0], all_recv.at[1])
    added = make_deposit(0)
    all_wait(mass_in.at[0], all_recv.at[3])
    turn_back(mass_in.at[0], 0, added, 1, 4)
    all_wait(tile_in.at[1], all_recv.at[2])
    added = make_deposit(1)
    all_wait(mass_in.at[1], all_recv.at[4])
    for f in range(planes):
        held_mass[f] = unfold(mass_in[1, :, f, :])
    mass = held_mass[...]
    second_edges = mass_edges(4, mass)
    for copy in second_edges:
        copy.start()
    for copy in second_edges:
        copy.wait()
    send_mass(advance(mass, 4), 2, 5)
    all_wait(mass_in.at[2], all_recv.at[5])
    turn_back(mass_in.at[2], 1, added, 3, 6)
    all_wait(mass_in.at[3], all_recv.at[6])
    for f in range(planes):
        out_ref[f] = unfold(mass_in[3, :, f, :])
    all_wait(names_in, all_send.at[0])
    for number in range(steps):
        all_wait(tile_out.at[number], all_send.at[1 + number])
    for turn in range(4):
        all_wait(mass_out.at[turn], all_send.at[3 + turn])


def body(density, phi_speed, rad_speed, profile, tiles, owners, slots, shifts):
    fluids, layers, cells, width = density.shape
    planes = fluids * layers
    count = lax.axis_size("phi")
    per = width // count
    steps, held, strip = tiles.shape[:3]
    lanes = per * cells
    me = lax.axis_index("phi")
    shape = (planes, cells, width)
    mine = lax.dynamic_slice_in_dim(shifts.reshape(steps, per, count), me, 1, axis=2)[:, :, 0]
    whole = mine // cells
    rest = jnp.repeat(mine % cells, cells, axis=1)
    names = jnp.stack([owners[:, :, 0], slots], axis=1).astype(jnp.float32)
    names = jnp.tile(names, (1, 1, per)).reshape(1, 2 * steps, lanes)
    smem, vmem = pl.BlockSpec(memory_space=pltpu.SMEM), pl.BlockSpec(memory_space=pltpu.VMEM)
    sent = 4 * count * lanes * (4 * planes + 2 * strip + 4)
    out = pl.pallas_call(
        fused,
        out_shape=jax.ShapeDtypeStruct(shape, jnp.float32),
        in_specs=[smem] * 2 + [vmem] * 6,
        out_specs=vmem,
        scratch_shapes=[
            pltpu.VMEM((10, 8, 128), jnp.float32),
            pltpu.VMEM((10, 8, 128), jnp.float32),
            pltpu.VMEM((count, 2 * steps, lanes), jnp.float32),
            pltpu.VMEM((steps, count, strip, lanes), jnp.float32),
            pltpu.VMEM((steps, count, strip, lanes), jnp.float32),
            pltpu.VMEM((4, count, planes, lanes), jnp.float32),
            pltpu.VMEM((4, count, planes, lanes), jnp.float32),
            pltpu.VMEM((2 * count + 1, planes, lanes), jnp.float32),
            pltpu.VMEM(shape, jnp.float32),
            pltpu.VMEM((lanes, 2 * lanes), jnp.bfloat16),
            pltpu.VMEM((3 * cells, 2 * lanes), jnp.bfloat16),
            pltpu.VMEM((lanes, 3 * cells), jnp.float32),
            pltpu.SemaphoreType.DMA((10,)),
            pltpu.SemaphoreType.DMA((10,)),
            pltpu.SemaphoreType.DMA((7,)),
            pltpu.SemaphoreType.DMA((7,)),
        ],
        compiler_params=pltpu.CompilerParams(
            collective_id=0, has_side_effects=True, vmem_limit_bytes=48 * 1024 * 1024
        ),
        cost_estimate=pl.CostEstimate(flops=10**9, bytes_accessed=sent, transcendentals=0),
    )(
        whole,
        profile,
        rest,
        names,
        density.reshape(shape),
        phi_speed.reshape(shape),
        rad_speed.reshape(shape),
        tiles,
    )
    return out.reshape(density.shape)


def solution(mesh):
    placed = (
        P(None, None, "phi", "row"),
        P(None, None, "phi", "row"),
        P(None, None, "phi", "row"),
        P(),
        P(None, "phi", None, "row"),
        P(None, "phi", None),
        P(None, "phi"),
        P(None, "row"),
    )
    return jax.shard_map(
        body, mesh=mesh, in_specs=placed, out_specs=P(None, None, "phi", "row"), check_vma=False
    )
```

profile of v0, /device:TPU:1, one launch (start us, length us, event | category | flops | bytes accessed | tf_op | source)
XLA Modules:
  0.0 108.6 jit_solution(5192996185030177409)
XLA Ops:
  0.0 0.0 copy-start.7
  0.0 0.0 copy-start.6
  0.0 0.7 copy-done.7
  0.7 0.0 copy-done.6
  0.7 0.0 copy-start.5
  0.7 0.1 tile.9.names_ref
  0.8 0.6 copy-done.5
  1.4 0.1 reshape.40
  1.5 0.1 constant_dynamic-slice_fusion
  1.5 0.1 copy.11
  1.7 0.1 broadcast_in_dim.3
  1.7 0.0 copy-start.4
  1.7 0.1 reshape.41.rest_ref
  1.8 0.6 copy-done.4
  2.4 0.0 copy-start
  2.4 1.0 copy-done
  3.4 0.0 copy-start.1
  3.4 0.9 copy-done.1
  4.4 0.0 copy-start.2
  4.4 0.9 copy-done.2
  5.3 0.0 copy-start.3
  5.3 0.9 copy-done.3
  6.2 101.7 %shard_map.82 = f32[6,64,128]{2,1,0:T(8,128)S(1)} custom-call(s32[2,2]{1,0:T(2,128)S(1)} %get-tuple-element.6.whole_ref, f32[2]{0:T(128)S(1)} %copy-done.4, s32[2,128]{1,0:T(2,128)S(1)} %reshape.41.rest_ref, f32[1,4,128]{2,1,0:T(4,128)S(1)} %tile.9.names_ref, f32[6,64,128]{2,1,0:T(8,128)S(1)} %bitcast.29, f32[6,64,128]{2,1,0:T(8,128)S(1)} %bitcast.30, ...), custom_call_target="tpu_custom_call" | custom-call | flops 1000000000 | bytes 1441792 | tf_op jit(solution)/shard_map/pallas_call | solution.py:280
  107.9 0.7 copy.13
  (4 shorter events, 0.0 us)
Async XLA Ops:
  0.0 0.7 copy-start.7
  0.0 0.7 copy-start.6
  0.7 0.7 copy-start.5
  1.7 0.7 copy-start.4
  2.4 1.0 copy-start
  3.4 0.9 copy-start.1
  4.4 0.9 copy-start.2
  5.3 0.9 copy-start.3
where the time goes:
time: 109 us
  Pallas kernels  102 us (94%)
  local copies, waits for them, and re-layouts  6.86 us (6%)
    pallas_call x1, Pallas kernels, body(): pl.pallas_call(fused, out_shape=jax.ShapeDtypeStruct(shape, jnp.float32),...  102 us
    unnamed x18, local copies, waits for them, and re-layouts  6.46 us

commit v1 on v0

--- a/solution.py
+++ b/solution.py
@@ -24,19 +24,26 @@
     profile_ref,
     rest_ref,
     names_ref,
+    mass_hbm,
+    phi_hbm,
+    rad_hbm,
+    tiles_hbm,
+    out_ref,
     mass_ref,
     phi_ref,
     rad_ref,
     tiles_ref,
-    out_ref,
     edge_out,
     edge_in,
     names_in,
     tile_out,
     tile_in,
-    mass_out,
-    mass_in,
-    twice,
+    gas_out,
+    gas_in,
+    gas_twice,
+    dust_out,
+    dust_in,
+    dust_twice,
     held_mass,
     lhs,
     rhs,
@@ -45,6 +52,7 @@
     edge_recv,
     all_send,
     all_recv,
+    load,
 ):
     planes, cells, width = mass_ref.shape
     steps = tiles_ref.shape[0]
@@ -56,7 +64,23 @@
     up, down = lax.rem(me + 1, count), lax.rem(me + count - 1, count)
     outward, inward = lax.rem(row + 1, row_count), lax.rem(row + row_count - 1, row_count)
 
+    layers = profile_ref.shape[0]
+    gas = (0, layers, gas_out, gas_in, gas_twice)
+    dust = (layers, planes - layers, dust_out, dust_in, dust_twice)
+    loads = [
+        pltpu.make_async_copy(source, target, load.at[n])
+        for n, (source, target) in enumerate(
+            ((mass_hbm, mass_ref), (phi_hbm, phi_ref), (rad_hbm, rad_ref), (tiles_hbm, tiles_ref))
+        )
+    ]
+    for copy in loads:
+        copy.start()
+
     barrier = pltpu.get_barrier_semaphore()
+
+    def peer_of(step):
+        near = step // 2
+        return lax.rem(me + count // 2 + near * (2 * lax.rem(step, 2) - 1), count)
 
     @pl.loop(1, count)
     def _(step):
@@ -66,11 +90,11 @@
     pl.semaphore_signal(barrier, inc=1, device_id={"row": inward}, device_id_type=MESH)
 
     def put_column(place, field, column):
-        rows = [field[f].T[column : column + 1, :] for f in range(planes)]
-        edge_out[place, :planes, :cells] = jnp.concatenate(rows, axis=0)
+        rows = [field[f].T[column : column + 1, :] for f in range(field.shape[0])]
+        edge_out[place, : field.shape[0], :cells] = jnp.concatenate(rows, axis=0)
 
     def put_row(place, field, at):
-        edge_out[place, :planes, :width] = field[:, at, :]
+        edge_out[place, : field.shape[0], :width] = field[:, at, :]
 
     def edge(place, target):
         return pltpu.make_async_remote_copy(
@@ -97,7 +121,7 @@
     def send_all(source, target, number):
         @pl.loop(1, count)
         def _(step):
-            peer = lax.rem(me + step, count)
+            peer = peer_of(step)
             pltpu.make_async_remote_copy(
                 src_ref=source.at[peer],
                 dst_ref=target.at[me],
@@ -113,11 +137,14 @@
         others = target.at[pl.ds(0, count - 1)]
         pltpu.make_async_copy(others, others, semaphore).wait()
 
+    loads[0].wait()
     density = mass_ref[...]
     first_edges = mass_edges(0, density)
-    put_row(8, phi_ref, 0)
-    put_column(9, rad_ref, 0)
-    first_edges += [edge(8, {"phi": down}), edge(9, {"row": inward})]
+    loads[1].wait()
+    loads[2].wait()
+    put_row(12, phi_ref, 0)
+    put_column(13, rad_ref, 0)
+    first_edges += [edge(12, {"phi": down}), edge(13, {"row": inward})]
     names_in[pl.ds(me, 1)] = names_ref[...]
 
     pl.semaphore_wait(barrier, count + 1)
@@ -131,7 +158,7 @@
             dst_ref=names_in.at[me],
             send_sem=all_send.at[0],
             recv_sem=all_recv.at[0],
-            device_id={"phi": lax.rem(me + step, count)},
+            device_id={"phi": peer_of(step)},
             device_id_type=MESH,
         ).start()
 
@@ -140,41 +167,45 @@
             tile_out[number, :, p, :] = fold(tiles_ref[number, :, p, :])
         send_all(tile_out.at[number], tile_in.at[number], 1 + number)
 
-    send_tiles(0)
+    loads[3].wait()
 
     lane = lax.broadcasted_iota(jnp.int32, (1, 1, width), 2)
     cell = lax.broadcasted_iota(jnp.int32, (1, cells, 1), 1)
 
-    def rows_of(place):
-        return edge_in[place, :planes, :width].reshape(planes, 1, width)
-
-    def columns_of(place, outside):
+    def rows_of(place, start, size):
+        return edge_in[place, start : start + size, :width].reshape(size, 1, width)
+
+    def columns_of(place, start, size, outside):
         turned = edge_in[place].T
-        found = jnp.stack([turned[:cells, f : f + 1] for f in range(planes)], axis=0)
+        found = jnp.stack([turned[:cells, f : f + 1] for f in range(start, start + size)], axis=0)
         return jnp.where(outside, 0.0, found)
 
     for copy in first_edges:
         copy.wait()
-    speed_phi, speed_rad = phi_ref[...], rad_ref[...]
-    speed_next = jnp.where(cell == cells - 1, rows_of(8), pltpu.roll(speed_phi, cells - 1, 1))
     last_row = row == row_count - 1
-    radial_next = jnp.where(lane == width - 1, columns_of(9, last_row), pltpu.roll(speed_rad, width - 1, 2))
-
-    def advance(mass, base):
-        behind = jnp.where(cell == 0, rows_of(base), pltpu.roll(mass, 1, 1))
-        ahead = jnp.where(cell == cells - 1, rows_of(base + 1), pltpu.roll(mass, cells - 1, 1))
-        inner = jnp.where(lane == 0, columns_of(base + 2, row == 0), pltpu.roll(mass, 1, 2))
-        outer = jnp.where(lane == width - 1, columns_of(base + 3, last_row), pltpu.roll(mass, width - 1, 2))
+
+    def advance(group, mass, base, start):
+        first, size = group[:2]
+        speed_phi, speed_rad = phi_ref[first : first + size], rad_ref[first : first + size]
+        speed_next = jnp.where(cell == cells - 1, rows_of(12, first, size), pltpu.roll(speed_phi, cells - 1, 1))
+        rim = columns_of(13, first, size, last_row)
+        radial_next = jnp.where(lane == width - 1, rim, pltpu.roll(speed_rad, width - 1, 2))
+        behind = jnp.where(cell == 0, rows_of(base, start, size), pltpu.roll(mass, 1, 1))
+        ahead = jnp.where(cell == cells - 1, rows_of(base + 1, start, size), pltpu.roll(mass, cells - 1, 1))
+        inner = jnp.where(lane == 0, columns_of(base + 2, start, size, row == 0), pltpu.roll(mass, 1, 2))
+        rim = columns_of(base + 3, start, size, last_row)
+        outer = jnp.where(lane == width - 1, rim, pltpu.roll(mass, width - 1, 2))
         flux_in = jnp.maximum(speed_phi, 0.0) * behind + jnp.minimum(speed_phi, 0.0) * mass
         flux_out = jnp.maximum(speed_next, 0.0) * mass + jnp.minimum(speed_next, 0.0) * ahead
         radial_in = jnp.maximum(speed_rad, 0.0) * inner + jnp.minimum(speed_rad, 0.0) * mass
         radial_out = jnp.maximum(radial_next, 0.0) * mass + jnp.minimum(radial_next, 0.0) * outer
         return mass - (flux_out - flux_in) - (radial_out - radial_in)
 
-    def send_mass(mass, turn, number):
-        for f in range(planes):
+    def send_mass(group, mass, turn, channel):
+        first, size, mass_out, mass_in, twice = group
+        for f in range(size):
             mass_out[turn, :, f, :] = fold(mass[f])
-        send_all(mass_out.at[turn], mass_in.at[turn], number)
+        send_all(mass_out.at[turn], mass_in.at[turn], channel + turn)
 
     def make_deposit(number):
         line = lax.broadcasted_iota(jnp.int32, (lanes, lanes), 0)
@@ -211,11 +242,13 @@
     spot = lax.broadcasted_iota(jnp.int32, (1, 1, lanes), 2)
     inside = lax.rem(spot, cells)
 
-    def turn_back(source, number, added, turn, channel):
-        for f in range(planes):
-            block = source[:, f, :]
-            if f < profile_ref.shape[0]:
-                block = block + profile_ref[f] * added
+    def turn_back(group, number, added, turn, channel):
+        first, size, mass_out, mass_in, twice = group
+        all_wait(mass_in.at[turn - 1], all_recv.at[channel + turn - 1])
+        for f in range(size):
+            block = mass_in[turn - 1, :, f, :]
+            if first + f < layers:
+                block = block + profile_ref[first + f] * added
             twice[pl.ds(1, count), f, :] = block
             twice[pl.ds(1 + count, count), f, :] = block
             twice[0, f : f + 1, :] = block[count - 1 :]
@@ -226,39 +259,60 @@
         mixed = jnp.where(inside < cells - rest, here, prev)
         moved = inside - rest
         index = (spot - inside) + jnp.where(moved < 0, moved + cells, moved)
-        index = jnp.broadcast_to(index, mixed.shape).reshape(count * planes, lanes)
-        mass_out[turn] = jnp.take_along_axis(mixed.reshape(count * planes, lanes), index, axis=1).reshape(mixed.shape)
-        send_all(mass_out.at[turn], mass_in.at[turn], channel)
-
-    send_mass(advance(density, 0), 0, 3)
-    send_tiles(1)
+        index = jnp.broadcast_to(index, mixed.shape).reshape(count * size, lanes)
+        mass_out[turn] = jnp.take_along_axis(mixed.reshape(count * size, lanes), index, axis=1).reshape(mixed.shape)
+        send_all(mass_out.at[turn], mass_in.at[turn], channel + turn)
+
+    def regain(group, turn, channel, target, start):
+        first, size, mass_out, mass_in, twice = group
+        all_wait(mass_in.at[turn], all_recv.at[channel + turn])
+        for f in range(size):
+            target[start + f] = unfold(mass_in[turn, :, f, :])
+
+    def begin_edges(group, base):
+        first, size = group[:2]
+        copies = mass_edges(base, held_mass[first : first + size])
+        for copy in copies:
+            copy.start()
+        return copies
+
+    def second(group, copies, base, channel):
+        first, size = group[:2]
+        for copy in copies:
+            copy.wait()
+        send_mass(group, advance(group, held_mass[first : first + size], base, 0), 2, channel)
+
+    def first_half(group, channel):
+        first, size = group[:2]
+        send_mass(group, advance(group, mass_ref[first : first + size], 0, first), 0, channel)
+
+    first_half(dust, 3)
+    send_tiles(0)
+    first_half(gas, 7)
+    turn_back(dust, 0, None, 1, 3)
     all_wait(names_in, all_recv.at[0])
     all_wait(tile_in.at[0], all_recv.at[1])
     added = make_deposit(0)
-    all_wait(mass_in.at[0], all_recv.at[3])
-    turn_back(mass_in.at[0], 0, added, 1, 4)
+    turn_back(gas, 0, added, 1, 7)
+    send_tiles(1)
+    regain(dust, 1, 3, held_mass, dust[0])
+    dust_edges = begin_edges(dust, 4)
+    regain(gas, 1, 7, held_mass, gas[0])
+    gas_edges = begin_edges(gas, 8)
+    second(dust, dust_edges, 4, 3)
+    second(gas, gas_edges, 8, 7)
     all_wait(tile_in.at[1], all_recv.at[2])
     added = make_deposit(1)
-    all_wait(mass_in.at[1], all_recv.at[4])
-    for f in range(planes):
-        held_mass[f] = unfold(mass_in[1, :, f, :])
-    mass = held_mass[...]
-    second_edges = mass_edges(4, mass)
-    for copy in second_edges:
-        copy.start()
-    for copy in second_edges:
-        copy.wait()
-    send_mass(advance(mass, 4), 2, 5)
-    all_wait(mass_in.at[2], all_recv.at[5])
-    turn_back(mass_in.at[2], 1, added, 3, 6)
-    all_wait(mass_in.at[3], all_recv.at[6])
-    for f in range(planes):
-        out_ref[f] = unfold(mass_in[3, :, f, :])
+    turn_back(dust, 1, None, 3, 3)
+    turn_back(gas, 1, added, 3, 7)
+    regain(dust, 3, 3, out_ref, dust[0])
+    regain(gas, 3, 7, out_ref, gas[0])
     all_wait(names_in, all_send.at[0])
     for number in range(steps):
         all_wait(tile_out.at[number], all_send.at[1 + number])
-    for turn in range(4):
-        all_wait(mass_out.at[turn], all_send.at[3 + turn])
+    for group, channel in ((dust, 3), (gas, 7)):
+        for turn in range(4):
+            all_wait(group[2].at[turn], all_send.at[channel + turn])
 
 
 def body(density, phi_speed, rad_speed, profile, tiles, owners, slots, shifts):
@@ -280,28 +334,36 @@
     out = pl.pallas_call(
         fused,
         out_shape=jax.ShapeDtypeStruct(shape, jnp.float32),
-        in_specs=[smem] * 2 + [vmem] * 6,
+        in_specs=[smem] * 2 + [vmem] * 2 + [pl.BlockSpec(memory_space=pltpu.HBM)] * 4,
         out_specs=vmem,
         scratch_shapes=[
-            pltpu.VMEM((10, 8, 128), jnp.float32),
-            pltpu.VMEM((10, 8, 128), jnp.float32),
+            pltpu.VMEM(shape, jnp.float32),
+            pltpu.VMEM(shape, jnp.float32),
+            pltpu.VMEM(shape, jnp.float32),
+            pltpu.VMEM(tiles.shape, jnp.float32),
+            pltpu.VMEM((14, 8, 128), jnp.float32),
+            pltpu.VMEM((14, 8, 128), jnp.float32),
             pltpu.VMEM((count, 2 * steps, lanes), jnp.float32),
             pltpu.VMEM((steps, count, strip, lanes), jnp.float32),
             pltpu.VMEM((steps, count, strip, lanes), jnp.float32),
-            pltpu.VMEM((4, count, planes, lanes), jnp.float32),
-            pltpu.VMEM((4, count, planes, lanes), jnp.float32),
-            pltpu.VMEM((2 * count + 1, planes, lanes), jnp.float32),
+            pltpu.VMEM((4, count, layers, lanes), jnp.float32),
+            pltpu.VMEM((4, count, layers, lanes), jnp.float32),
+            pltpu.VMEM((2 * count + 1, layers, lanes), jnp.float32),
+            pltpu.VMEM((4, count, planes - layers, lanes), jnp.float32),
+            pltpu.VMEM((4, count, planes - layers, lanes), jnp.float32),
+            pltpu.VMEM((2 * count + 1, planes - layers, lanes), jnp.float32),
             pltpu.VMEM(shape, jnp.float32),
             pltpu.VMEM((lanes, 2 * lanes), jnp.bfloat16),
             pltpu.VMEM((3 * cells, 2 * lanes), jnp.bfloat16),
             pltpu.VMEM((lanes, 3 * cells), jnp.float32),
-            pltpu.SemaphoreType.DMA((10,)),
-            pltpu.SemaphoreType.DMA((10,)),
-            pltpu.SemaphoreType.DMA((7,)),
-            pltpu.SemaphoreType.DMA((7,)),
+            pltpu.SemaphoreType.DMA((14,)),
+            pltpu.SemaphoreType.DMA((14,)),
+            pltpu.SemaphoreType.DMA((11,)),
+            pltpu.SemaphoreType.DMA((11,)),
+            pltpu.SemaphoreType.DMA((4,)),
         ],
         compiler_params=pltpu.CompilerParams(
-            collective_id=0, has_side_effects=True, vmem_limit_bytes=48 * 1024 * 1024
+            collective_id=0, has_side_effects=True, vmem_limit_bytes=67043328
         ),
         cost_estimate=pl.CostEstimate(flops=10**9, bytes_accessed=sent, transcendentals=0),
     )(

time: 109 us -> 102 us (0.936)
  Pallas kernels: 102 us -> 97.1 us
  local copies, waits for them, and re-layouts: 6.86 us -> 3.98 us
    pallas_call x1, Pallas kernels: 102 us -> 97.1 us  [body(): pl.pallas_call(fused, out_shape=jax.ShapeDtypeStruct(shape, jnp.float32),...]
    unnamed x18 -> x8, local copies, waits for them, and re-layouts: 6.46 us -> 2.42 us
where the time goes in v1:
time: 102 us
  Pallas kernels  97.1 us (95%)
  local copies, waits for them, and re-layouts  3.98 us (4%)
    pallas_call x1, Pallas kernels, body(): pl.pallas_call(fused, out_shape=jax.ShapeDtypeStruct(shape, jnp.float32),...  97.1 us
    unnamed x8, local copies, waits for them, and re-layouts  2.42 us

profile of v1, /device:TPU:1, one launch (start us, length us, event | category | flops | bytes accessed | tf_op | source)
XLA Modules:
  0.0 101.7 jit_solution(13690853868414388964)
XLA Ops:
  0.0 0.0 copy-start.2
  0.0 0.0 copy-start.1
  0.0 0.7 copy-done.2
  0.7 0.0 copy-done.1
  0.7 0.0 copy-start
  0.7 0.7 tile.9.names_ref
  1.4 0.0 copy-done
  1.4 0.1 reshape.40
  1.5 0.1 constant_dynamic-slice_fusion
  1.5 0.1 copy.11
  1.7 0.6 and_select_fusion
  2.2 0.1 broadcast_in_dim.3
  2.3 0.7 reshape.41.rest_ref
  3.0 97.1 %shard_map.82 = f32[6,64,128]{2,1,0:T(8,128)} custom-call(s32[2,2]{1,0:T(2,128)} %get-tuple-element.6.whole_ref, f32[2]{0:T(128)} %profile_ref.1, s32[2,128]{1,0:T(2,128)} %reshape.41.rest_ref, f32[1,4,128]{2,1,0:T(4,128)} %tile.9.names_ref, f32[6,64,128]{2,1,0:T(8,128)} %bitcast.31, f32[6,64,128]{2,1,0:T(8,128)} %bitcast.32, f32[6,64,128]{2,1,0:T(8,128)} %bitcast.33, ...), custom_call_target="tpu_custom_call" | custom-call | flops 1000000000 | bytes 1441792 | tf_op jit(solution)/shard_map/pallas_call | solution.py:334
  100.1 1.6 %copy.13 = f32[3,2,64,128]{3,2,1,0:T(8,128)} copy(f32[3,2,64,128]{3,2,1,0:T(8,128)} %bitcast.28) | data formatting | bytes 393216
  (3 shorter events, 0.0 us)
Async XLA Ops:
  0.0 0.7 copy-start.2
  0.0 0.7 copy-start.1
  0.7 0.7 copy-start

commit v2 on v1

--- a/solution.py
+++ b/solution.py
@@ -219,8 +219,10 @@
         def _(pair):
             for side in range(2):
                 source = 2 * pair + side
-                names = names_in[source]
-                own, slot = names[2 * number : 2 * number + 1], names[2 * number + 1 : 2 * number + 2]
+                name = names_in[source][:, number * cells : (number + 1) * cells]
+                name = jnp.concatenate([name, name], axis=1)
+                own = jnp.floor(name * (1.0 / places))
+                slot = name - own * places
                 block = tile_in[number, source]
                 high = block.astype(jnp.bfloat16).astype(jnp.float32)
                 left = block - high
@@ -327,10 +329,9 @@
     mine = lax.dynamic_slice_in_dim(shifts.reshape(steps, per, count), me, 1, axis=2)[:, :, 0]
     whole = mine // cells
     rest = jnp.repeat(mine % cells, cells, axis=1)
-    names = jnp.stack([owners[:, :, 0], slots], axis=1).astype(jnp.float32)
-    names = jnp.tile(names, (1, 1, per)).reshape(1, 2 * steps, lanes)
+    names = (owners[:, :, 0] * (cells // strip) + slots).astype(jnp.float32).reshape(1, 1, lanes)
     smem, vmem = pl.BlockSpec(memory_space=pltpu.SMEM), pl.BlockSpec(memory_space=pltpu.VMEM)
-    sent = 4 * count * lanes * (4 * planes + 2 * strip + 4)
+    sent = 4 * count * lanes * (4 * planes + 2 * strip + 1)
     out = pl.pallas_call(
         fused,
         out_shape=jax.ShapeDtypeStruct(shape, jnp.float32),
@@ -343,7 +344,7 @@
             pltpu.VMEM(tiles.shape, jnp.float32),
             pltpu.VMEM((14, 8, 128), jnp.float32),
             pltpu.VMEM((14, 8, 128), jnp.float32),
-            pltpu.VMEM((count, 2 * steps, lanes), jnp.float32),
+            pltpu.VMEM((count, 1, lanes), jnp.float32),
             pltpu.VMEM((steps, count, strip, lanes), jnp.float32),
             pltpu.VMEM((steps, count, strip, lanes), jnp.float32),
             pltpu.VMEM((4, count, layers, lanes), jnp.float32),

time: 102 us -> 105 us (1.029)
  Pallas kernels: 97.1 us -> 99.7 us
    pallas_call x1, Pallas kernels: 97.1 us -> 99.7 us  [body(): pl.pallas_call(fused, out_shape=jax.ShapeDtypeStruct(shape, jnp.float32),...]
where the time goes in v2:
time: 105 us
  Pallas kernels  99.7 us (95%)
  local copies, waits for them, and re-layouts  4.63 us (4%)
    pallas_call x1, Pallas kernels, body(): pl.pallas_call(fused, out_shape=jax.ShapeDtypeStruct(shape, jnp.float32),...  99.7 us
    unnamed x8, local copies, waits for them, and re-layouts  3.14 us

profile of v2, /device:TPU:1, one launch (start us, length us, event | category | flops | bytes accessed | tf_op | source)
XLA Modules:
  0.0 104.9 jit_solution(746768149532950822)
XLA Ops:
  0.0 0.0 copy-start.2
  0.0 0.7 copy-done.2
  0.7 0.0 copy-start
  0.7 0.7 copy-done
  1.4 0.0 copy-start.1
  1.4 0.6 reshape.25.names_ref
  2.0 0.1 copy-done.1
  2.0 0.1 reshape.23
  2.1 0.1 constant_dynamic-slice_fusion
  2.2 0.1 copy.10
  2.3 0.6 and_select_fusion
  2.9 0.1 broadcast_in_dim.3
  3.0 0.7 reshape.24.rest_ref
  3.6 99.7 %shard_map.82 = f32[6,64,128]{2,1,0:T(8,128)} custom-call(s32[2,2]{1,0:T(2,128)} %get-tuple-element.6.whole_ref, f32[2]{0:T(128)} %profile_ref.1, s32[2,128]{1,0:T(2,128)} %reshape.24.rest_ref, f32[1,1,128]{2,1,0:T(1,128)} %reshape.25.names_ref, f32[6,64,128]{2,1,0:T(8,128)} %bitcast.27, f32[6,64,128]{2,1,0:T(8,128)} %bitcast.28, f32[6,64,128]{2,1,0:T(8,128)} %bitcast.29, ...), custom_call_target="tpu_custom_call" | custom-call | flops 1000000000 | bytes 1343488 | tf_op jit(solution)/shard_map/pallas_call | solution.py:335
  103.3 1.6 %copy.12 = f32[3,2,64,128]{3,2,1,0:T(8,128)} copy(f32[3,2,64,128]{3,2,1,0:T(8,128)} %bitcast.25) | data formatting | bytes 393216
  (2 shorter events, 0.0 us)
Async XLA Ops:
  0.0 0.7 copy-start.2
  0.7 0.7 copy-start
  1.4 0.7 copy-start.1
